TPU v7x, 32 devices: a whole 2x2x4 slice. The times are simulated.
32 devices in a mesh: dp: 4 (over y, core), mp: 8 (over z, x).
Axes of the slice: x: 2, y: 2, z: 4, core: 2. Of those that a mesh axis runs over, the one named last changes fastest.
Arguments:
- gradient: float32 [8192, 16384], P(('dp', 'mp')), may hold values from -2000 to 2000
- left_basis: float32 [8192, 1024], P(('dp', 'mp')), may hold values from -1 to 1, as said below
- left_values: float32 [8192], P(('dp', 'mp')), may hold values from 0.05 to 2
- right_candidates: float32 [4, 16384, 256], P('dp', 'mp'), may hold values from -1 to 1, as said below
- right_owner: int32 [64], P('mp'), may hold values from 0 to 3
- right_values: float32 [16384], P('mp'), may hold values from 0.05 to 2
Outputs:
- direction: float32 [8192, 16384], P(('dp', 'mp'))
Inputs may be any that keep to these rules, and one draw needn't show every extreme that they name: Each block of 1024 rows of left_basis is an orthogonal 1024 x 1024 matrix. For every data group, each block of 256 rows of right_candidates is an orthogonal 256 x 256 matrix. right_owner[j] names the data group whose copy of column block j is current.
All inputs are finite; a program needn't handle non-finite values.
Results may differ from a plain program's by a relative error of at most 0.00011.
Values sent between devices are 32-bit elements; how exact they have to be, the bound alone decides.
A program may use at most 128 MiB of HBM per device.

v0:
```python
import functools

import jax
import jax.numpy as jnp
from jax import lax
from jax.experimental import pallas as pl
from jax.experimental.pallas import tpu as pltpu
from jax.sharding import PartitionSpec as P

BL = 1024
BR = 256
WINDOW = 5
HOOK = 3

damping = 0.01
epsilon = 1e-06

MESH = pl.DeviceIdType.MESH
F32 = jnp.float32
BF16 = jnp.bfloat16


def flip(index, mask):
    bit = 1
    while bit <= mask:
        if mask & bit:
            index = index + bit - 2 * bit * ((index // bit) % 2)
        bit *= 2
    return index


def halves(value):
    head = value.astype(BF16)
    return head, (value - head.astype(F32)).astype(BF16)


def product(a_head, a_tail, b_head, b_tail, dims):
    def dot(a, b):
        return lax.dot_general(a, b, (dims, ((), ())), preferred_element_type=F32)

    return dot(a_head, b_head) + (dot(a_head, b_tail) + dot(a_tail, b_head))


NN = ((1,), (0,))
NT = ((1,), (1,))


def kernel(
    n_dp, n_mp, rows, members, families, span, blocks,
    grad, left, lvals, cand, owner, rvals,
    out, total,
    inbuf, lfull, lh, ll, lth, ltl, lev, lvbuf, lam, chosen, parts, right, sqbuf, acc,
    in_send, in_recv, out_send, out_recv, own_in, own_out,
    l_send, l_recv, lv_send, lv_recv, rs_send, rs_recv, ag_send, ag_recv, sw_send, sw_recv,
    lam_send, lam_recv, sq_send, sq_recv, loc,
):
    dp = lax.axis_index("dp")
    mp = lax.axis_index("mp")
    seat = mp % members
    family = mp // members
    part_rows = span // n_dp
    count = families * blocks

    def member(k):
        return family * members + flip(seat, k)

    def cousin(s, sign):
        return ((family + sign * s + families) % families) * members + seat

    def remote(src, dst, send, recv, d, m):
        return pltpu.make_async_remote_copy(
            src_ref=src, dst_ref=dst, send_sem=send, recv_sem=recv,
            device_id=(d, m), device_id_type=MESH,
        )

    cand_copy = pltpu.make_async_copy(cand.at[0], chosen, loc.at[0])
    cand_copy.start()
    left_copy = pltpu.make_async_copy(
        left, lfull.at[pl.ds(pl.multiple_of(seat * rows, rows), rows), :], loc.at[1]
    )
    left_copy.start()
    lam_copy = pltpu.make_async_copy(rvals, lam.at[0], loc.at[2])
    lam_copy.start()
    lv_copy = pltpu.make_async_copy(lvals, lvbuf.at[seat], loc.at[3])
    lv_copy.start()

    def column(c, who):
        s, j = c // blocks, c % blocks
        col = (((family + s) % families) * members + who) * span + j * BR
        return pl.ds(pl.multiple_of(col, BR), BR)

    def row_part(who):
        return pl.ds(pl.multiple_of(who * rows, rows), rows)

    def own_in_copy(c):
        return pltpu.make_async_copy(
            grad.at[:, column(c, seat)], inbuf.at[c, row_part(seat), :], own_in.at[c]
        )

    def in_copy(c, k):
        return remote(
            grad.at[:, column(c, flip(seat, k))], inbuf.at[c, row_part(seat), :],
            in_send.at[c, k - 1], in_recv.at[c, k - 1], dp, member(k),
        )

    def in_arrival(c, k):
        who = flip(seat, k)
        return remote(
            grad.at[:, column(c, seat)], inbuf.at[c, row_part(who), :],
            in_send.at[c, k - 1], in_recv.at[c, k - 1], dp, member(k),
        )

    def out_copy(c, k):
        who = flip(seat, k)
        return remote(
            inbuf.at[c, row_part(who), :], out.at[:, column(c, seat)],
            out_send.at[c, k - 1], out_recv.at[c, k - 1], dp, member(k),
        )

    def out_arrival(c, k):
        who = flip(seat, k)
        return remote(
            inbuf.at[c, row_part(who), :], out.at[:, column(c, who)],
            out_send.at[c, k - 1], out_recv.at[c, k - 1], dp, member(k),
        )

    def own_out_copy(c):
        return pltpu.make_async_copy(
            inbuf.at[c, row_part(seat), :], out.at[:, column(c, seat)], own_out.at[c]
        )

    partners = [(0, k) for k in range(1, members)]
    barrier = pltpu.get_barrier_semaphore()
    greeted = 0
    for k in range(1, members):
        pl.semaphore_signal(barrier, inc=1, device_id=(dp, member(k)), device_id_type=MESH)
        greeted += 1
    for s in range(1, families):
        pl.semaphore_signal(barrier, inc=1, device_id=(dp, cousin(s, 1)), device_id_type=MESH)
        greeted += 1
    for e in range(1, n_dp):
        pl.semaphore_signal(barrier, inc=1, device_id=(flip(dp, e), mp), device_id_type=MESH)
        greeted += 1
    pl.semaphore_wait(barrier, greeted)

    bits = []
    bit = 1
    while bit < members:
        bits.append(bit)
        bit *= 2
    orders = (bits, bits[::-1])
    half_rows = rows // 2

    def l_rows(who, half):
        start = who * rows + half * half_rows
        return pl.ds(pl.multiple_of(start, half_rows), half_rows)

    def l_round(half, r):
        order = orders[half]
        pieces = []
        for i in range(2 ** r):
            mask = 0
            for b in range(r):
                if i & (1 << b):
                    mask |= order[b]
            pieces.append((2 ** r - 1 + i, mask))
        return order[r], pieces

    def l_copy(half, bit, slot, mask):
        who = flip(seat, mask)
        where = l_rows(who, half)
        if mask:
            src = lfull.at[where, :]
        else:
            src = left.at[pl.ds(half * half_rows, half_rows), :]
        return remote(
            src, lfull.at[where, :], l_send.at[half, slot], l_recv.at[half, slot],
            dp, member(bit),
        )

    def l_arrival(half, bit, slot, mask):
        where = l_rows(flip(seat, mask ^ bit), half)
        return remote(
            lfull.at[where, :], lfull.at[where, :], l_send.at[half, slot], l_recv.at[half, slot],
            dp, member(bit),
        )

    def l_start(r):
        for half in range(2):
            bit, pieces = l_round(half, r)
            for slot, mask in pieces:
                l_copy(half, bit, slot, mask).start()

    def l_wait(r):
        for half in range(2):
            bit, pieces = l_round(half, r)
            for slot, mask in pieces:
                l_arrival(half, bit, slot, mask).wait_recv()

    l_start(0)
    for k in range(1, members):
        remote(
            lvals, lvbuf.at[seat], lv_send.at[k - 1], lv_recv.at[k - 1], dp, member(k)
        ).start()
    for s in range(1, families):
        remote(
            rvals, lam.at[s], lam_send.at[s - 1], lam_recv.at[s - 1], dp, cousin(s, -1)
        ).start()

    cand_copy.wait()

    def keep(b, carry):
        here = pl.ds(pl.multiple_of(b * BR, BR), BR)
        chosen[here, :] = jnp.where(owner[b] == dp, chosen[here, :], 0.0)
        return carry

    lax.fori_loop(0, blocks, keep, 0)

    def part(d):
        return pl.ds(pl.multiple_of(d * part_rows, part_rows), part_rows)

    def rs_copy(e):
        other = flip(dp, e)
        return remote(
            chosen.at[part(other), :], parts.at[e - 1],
            rs_send.at[e - 1], rs_recv.at[e - 1], other, mp,
        )

    def ag_copy(s, e):
        other = flip(dp, e)
        return remote(
            right.at[s, part(dp), :], right.at[s, part(dp), :],
            ag_send.at[s, e - 1], ag_recv.at[s, e - 1], other, mp,
        )

    def ag_arrival(s, e):
        other = flip(dp, e)
        return remote(
            right.at[s, part(other), :], right.at[s, part(other), :],
            ag_send.at[s, e - 1], ag_recv.at[s, e - 1], other, mp,
        )

    def sw_copy(s):
        return remote(
            right.at[0, part(dp), :], right.at[s, part(dp), :],
            sw_send.at[s - 1], sw_recv.at[s - 1], dp, cousin(s, -1),
        )

    for e in range(1, n_dp):
        rs_copy(e).start()

    for r in range(len(bits)):
        if r + 1 < len(bits):
            l_wait(r)
            l_start(r + 1)

    first = min(WINDOW, count)

    def begin(c, carry):
        own_in_copy(c).start()
        for k in range(1, members):
            in_copy(c, k).start()
        return carry

    lax.fori_loop(0, first, begin, 0)

    for e in range(1, n_dp):
        rs_copy(e).wait_recv()
    share = chosen[part(dp), :]
    for e in range(1, n_dp):
        share = share + parts[e - 1]
    right[0, part(dp), :] = share
    for s in range(1, families):
        sw_copy(s).start()
    for e in range(1, n_dp):
        ag_copy(0, e).start()

    lv_copy.wait()
    for k in range(1, members):
        remote(
            lvals, lvbuf.at[flip(seat, k)], lv_send.at[k - 1], lv_recv.at[k - 1], dp, member(k)
        ).wait_recv()

    def spread(m, carry):
        row = jnp.broadcast_to(lvbuf[m], (128, rows))
        lev[row_part(m), :] = row.T + damping
        return carry

    lax.fori_loop(0, members, spread, 0)
    lam_copy.wait()
    for s in range(1, families):
        remote(
            rvals, lam.at[s], lam_send.at[s - 1], lam_recv.at[s - 1], dp, cousin(s, -1)
        ).wait_recv()

    left_copy.wait()
    if bits:
        l_wait(len(bits) - 1)

    def prepare(i, carry):
        here = pl.ds(pl.multiple_of(i * BR, BR), BR)
        head, tail = halves(lfull[here, :])
        lh[here, :] = head
        ll[here, :] = tail
        for j in range(BL // BR):
            cols = slice(j * BR, (j + 1) * BR)
            head, tail = halves(lfull[here, cols].T)
            lth[cols, here] = head
            ltl[cols, here] = tail
        return carry

    lax.fori_loop(0, BL // BR, prepare, 0)
    acc[...] = jnp.zeros_like(acc)

    for e in range(1, n_dp):
        ag_arrival(0, e).wait_recv()

    def step(c, carry):
        @pl.when(c + WINDOW < count)
        def _():
            begin(c + WINDOW, 0)

        for s in range(1, families):
            @pl.when(c == min(s * blocks - 1, HOOK + s - 1))
            def _():
                sw_copy(s).wait_recv()
                for e in range(1, n_dp):
                    ag_copy(s, e).start()

            @pl.when(c == s * blocks)
            def _():
                for e in range(1, n_dp):
                    ag_arrival(s, e).wait_recv()

        own_in_copy(c).wait()
        for k in range(1, members):
            in_arrival(c, k).wait_recv()
        s, j = c // blocks, c % blocks
        here = pl.ds(pl.multiple_of(j * BR, BR), BR)
        basis_head, basis_tail = halves(right[s, here, :])
        head, tail = halves(inbuf[c])
        rotated = product(lth[...], ltl[...], head, tail, NN)
        head, tail = halves(rotated)
        turned = product(head, tail, basis_head, basis_tail, NN)
        levels = jnp.concatenate([lev[...]] * (BR // 128), axis=1)
        scaled = turned / (levels + lam[s, :, here])
        acc[...] += jnp.sum((scaled * scaled).reshape(BL // 8, 8, BR), axis=0)
        head, tail = halves(scaled)
        restored = product(head, tail, basis_head, basis_tail, NT)
        head, tail = halves(restored)
        inbuf[c] = product(lh[...], ll[...], head, tail, NN)
        for k in range(1, members):
            out_copy(c, k).start()
        own_out_copy(c).start()
        return carry

    lax.fori_loop(0, count, step, 0)

    mine = acc[:, :128]
    for j in range(1, BR // 128):
        mine = mine + acc[:, j * 128 : (j + 1) * 128]
    turn = 0
    steps = []
    bit = 1
    while bit < n_dp:
        steps.append((flip(dp, bit), mp))
        bit *= 2
    bit = 1
    while bit < members:
        steps.append((dp, member(bit)))
        bit *= 2
    for d, m in steps:
        sqbuf[2 * turn] = mine
        copy = remote(
            sqbuf.at[2 * turn], sqbuf.at[2 * turn + 1], sq_send.at[turn], sq_recv.at[turn], d, m
        )
        copy.start()
        copy.wait_recv()
        mine = mine + sqbuf[2 * turn + 1]
        turn += 1
    sqbuf[2 * turn] = mine
    whole = mine
    for s in range(1, families):
        copy = remote(
            sqbuf.at[2 * turn], sqbuf.at[2 * turn + s],
            sq_send.at[turn + s - 1], sq_recv.at[turn + s - 1], dp, cousin(s, 1),
        )
        copy.start()
    for s in range(1, families):
        remote(
            sqbuf.at[2 * turn], sqbuf.at[2 * turn + s],
            sq_send.at[turn + s - 1], sq_recv.at[turn + s - 1], dp, cousin(s, 1),
        ).wait_recv()
        whole = whole + sqbuf[2 * turn + s]
    total[...] = whole

    def finish(c, carry):
        own_out_copy(c).wait()
        for k in range(1, members):
            in_copy(c, k).wait_send()
            out_copy(c, k).wait_send()
            out_arrival(c, k).wait_recv()
        return carry

    for r in range(len(bits)):
        for half in range(2):
            bit, pieces = l_round(half, r)
            for slot, mask in pieces:
                l_copy(half, bit, slot, mask).wait_send()
    for k in range(1, members):
        remote(
            lvals, lvbuf.at[seat], lv_send.at[k - 1], lv_recv.at[k - 1], dp, member(k)
        ).wait_send()
    for s in range(1, families):
        remote(
            rvals, lam.at[s], lam_send.at[s - 1], lam_recv.at[s - 1], dp, cousin(s, -1)
        ).wait_send()
        sw_copy(s).wait_send()
        remote(
            sqbuf.at[2 * turn], sqbuf.at[2 * turn + s],
            sq_send.at[turn + s - 1], sq_recv.at[turn + s - 1], dp, cousin(s, 1),
        ).wait_send()
    for e in range(1, n_dp):
        rs_copy(e).wait_send()
        for s in range(families):
            ag_copy(s, e).wait_send()
    for i, (d, m) in enumerate(steps):
        remote(
            sqbuf.at[2 * i], sqbuf.at[2 * i + 1], sq_send.at[i], sq_recv.at[i], d, m
        ).wait_send()
    lax.fori_loop(0, count, finish, 0)


def solution(mesh):
    n_dp, n_mp = mesh.shape["dp"], mesh.shape["mp"]

    def on_device(gradient, left_basis, left_values, candidates, owner, right_values):
        rows, total_cols = gradient.shape
        members = BL // rows
        families = n_mp // members
        assert members * rows == BL and members * families == n_mp
        span = total_cols // n_mp
        blocks = span // BR
        count = families * blocks
        rounds = (n_dp - 1).bit_length() + (members - 1).bit_length()
        dma = pltpu.SemaphoreType.DMA
        many = max(members - 1, 1)
        others = max(families - 1, 1)
        anywhere = pl.BlockSpec(memory_space=pl.ANY)
        flops = 3 * 2 * BL * count * BR * (2 * BL + 2 * BR)
        raw, total = pl.pallas_call(
            functools.partial(kernel, n_dp, n_mp, rows, members, families, span, blocks),
            out_shape=(
                jax.ShapeDtypeStruct((rows, total_cols), F32),
                jax.ShapeDtypeStruct((8, 128), F32),
            ),
            in_specs=[
                anywhere, anywhere, anywhere, anywhere,
                pl.BlockSpec(memory_space=pltpu.SMEM), anywhere,
            ],
            out_specs=(anywhere, pl.BlockSpec(memory_space=pltpu.VMEM)),
            scratch_shapes=[
                pltpu.VMEM((count, BL, BR), F32),
                pltpu.VMEM((BL, BL), F32),
                pltpu.VMEM((BL, BL), BF16),
                pltpu.VMEM((BL, BL), BF16),
                pltpu.VMEM((BL, BL), BF16),
                pltpu.VMEM((BL, BL), BF16),
                pltpu.VMEM((BL, 128), F32),
                pltpu.VMEM((members, 1, rows), F32),
                pltpu.VMEM((families, 1, span), F32),
                pltpu.VMEM((span, BR), F32),
                pltpu.VMEM((n_dp - 1, span // n_dp, BR), F32),
                pltpu.VMEM((families, span, BR), F32),
                pltpu.VMEM((2 * rounds + families, 8, 128), F32),
                pltpu.VMEM((8, BR), F32),
                dma((count, many)), dma((count, many)), dma((count, many)), dma((count, many)),
                dma((count,)), dma((count,)),
                dma((2, many)), dma((2, many)), dma((many,)), dma((many,)),
                dma((n_dp - 1,)), dma((n_dp - 1,)),
                dma((families, n_dp - 1)), dma((families, n_dp - 1)),
                dma((others,)), dma((others,)), dma((others,)), dma((others,)),
                dma((rounds + others,)), dma((rounds + others,)),
                dma((4,)),
            ],
            compiler_params=pltpu.CompilerParams(
                collective_id=0, has_side_effects=True, vmem_limit_bytes=60 * 2**20
            ),
            cost_estimate=pl.CostEstimate(
                flops=flops, bytes_accessed=4 * rows * total_cols * 4, transcendentals=0
            ),
        )(
            gradient, left_basis, left_values.reshape(1, rows), candidates, owner,
            right_values.reshape(1, span),
        )
        mean_square = jnp.sum(total) / (rows * n_dp * n_mp * total_cols)
        return raw * lax.rsqrt(mean_square + epsilon)

    in_specs = (
        P(("dp", "mp"), None),
        P(("dp", "mp"), None),
        P(("dp", "mp")),
        P("dp", "mp", None),
        P("mp"),
        P("mp"),
    )
    return jax.shard_map(
        on_device, mesh=mesh, in_specs=in_specs, out_specs=P(("dp", "mp"), None), check_vma=False
    )
```

profile of v0, /device:TPU:0, one launch (start us, length us, event | category | flops | bytes accessed | tf_op | source)
XLA Modules:
  0.0 435.6 jit_solution(16460598027657032369)
XLA Ops:
  0.0 422.1 %shard_map.64 = (f32[256,16384]{1,0:T(8,128)}, f32[8,128]{1,0:T(8,128)}) custom-call(f32[256,16384]{1,0:T(8,128)} %grad.1, f32[256,1024]{1,0:T(8,128)} %left.1, f32[1,256]{1,0:T(1,128)} %bitcast.3, f32[1,2048,256]{2,1,0:T(8,128)} %cand.1, s32[8]{0:T(128)} %owner.1, f32[1,2048]{1,0:T(1,128)} %bitcast.2), custom_call_target="tpu_custom_call" | custom-call | flops 64424509440 | bytes 67108864 | tf_op jit(solution)/shard_map/pallas_call | solution.py:451
  422.1 1.3 reduce_sum.9
  424.0 11.6 %broadcast_multiply_fusion = f32[256,16384]{1,0:T(8,128)} fusion(f32[256,16384]{1,0:T(8,128)} %get-tuple-element.7, f32[]{:T(128)S(6)} %rsqrt.3), kind=kLoop, calls=%fused_computation | loop fusion | flops 4194304 | bytes 33554436 | tf_op jit(solution)/shard_map/mul | solution.py:497
where the time goes:
time: 436 us
  Pallas kernels  422 us (97%)
  other arithmetic  12.8 us (3%)
    pallas_call x1, Pallas kernels, on_device(): pl.pallas_call(functools.partial(kernel, n_dp, n_mp, rows, members, famil...  422 us
    mul x1, other arithmetic, on_device(): return raw * lax.rsqrt(mean_square + epsilon)  11.6 us

commit v1 on v0

--- a/solution.py
+++ b/solution.py
@@ -9,8 +9,10 @@
 
 BL = 1024
 BR = 256
-WINDOW = 5
-HOOK = 3
+AHEAD = 4
+EARLY = 2
+HOOK = 2
+VMEM_MIB = 44
 
 damping = 0.01
 epsilon = 1e-06
@@ -48,9 +50,9 @@
 def kernel(
     n_dp, n_mp, rows, members, families, span, blocks,
     grad, left, lvals, cand, owner, rvals,
-    out, total,
-    inbuf, lfull, lh, ll, lth, ltl, lev, lvbuf, lam, chosen, parts, right, sqbuf, acc,
-    in_send, in_recv, out_send, out_recv, own_in, own_out,
+    out,
+    inbuf, lfull, lh, ll, lth, ltl, lev, lvbuf, lam, chosen, parts, right, sqbuf, acc, facbuf,
+    in_send, in_recv, out_send, out_recv, own_in,
     l_send, l_recv, lv_send, lv_recv, rs_send, rs_recv, ag_send, ag_recv, sw_send, sw_recv,
     lam_send, lam_recv, sq_send, sq_recv, loc,
 ):
@@ -124,12 +126,20 @@
             out_send.at[c, k - 1], out_recv.at[c, k - 1], dp, member(k),
         )
 
-    def own_out_copy(c):
-        return pltpu.make_async_copy(
-            inbuf.at[c, row_part(seat), :], out.at[:, column(c, seat)], own_out.at[c]
-        )
-
-    partners = [(0, k) for k in range(1, members)]
+    def each_peer(action):
+        @pl.when(dp % 2 == 0)
+        def _():
+            for k in range(1, members):
+                action(k)
+
+        @pl.when(dp % 2 == 1)
+        def _():
+            for k in range(members - 1, 0, -1):
+                action(k)
+
+    def give(c):
+        each_peer(lambda k: out_copy(c, k).start())
+
     barrier = pltpu.get_barrier_semaphore()
     greeted = 0
     for k in range(1, members):
@@ -149,11 +159,12 @@
         bits.append(bit)
         bit *= 2
     orders = (bits, bits[::-1])
-    half_rows = rows // 2
+    cut = rows // 4
+    l_parts = ((0, cut), (cut, rows - cut))
 
     def l_rows(who, half):
-        start = who * rows + half * half_rows
-        return pl.ds(pl.multiple_of(start, half_rows), half_rows)
+        first, size = l_parts[half]
+        return pl.ds(pl.multiple_of(who * rows + first, cut), size)
 
     def l_round(half, r):
         order = orders[half]
@@ -172,7 +183,7 @@
         if mask:
             src = lfull.at[where, :]
         else:
-            src = left.at[pl.ds(half * half_rows, half_rows), :]
+            src = left.at[pl.ds(*l_parts[half]), :]
         return remote(
             src, lfull.at[where, :], l_send.at[half, slot], l_recv.at[half, slot],
             dp, member(bit),
@@ -197,7 +208,15 @@
             for slot, mask in pieces:
                 l_arrival(half, bit, slot, mask).wait_recv()
 
+    def begin(c, carry):
+        own_in_copy(c).start()
+        each_peer(lambda k: in_copy(c, k).start())
+        return carry
+
     l_start(0)
+    early = min(EARLY, count)
+    first = min(AHEAD, count)
+    lax.fori_loop(0, early, begin, 0)
     for k in range(1, members):
         remote(
             lvals, lvbuf.at[seat], lv_send.at[k - 1], lv_recv.at[k - 1], dp, member(k)
@@ -254,16 +273,6 @@
             l_wait(r)
             l_start(r + 1)
 
-    first = min(WINDOW, count)
-
-    def begin(c, carry):
-        own_in_copy(c).start()
-        for k in range(1, members):
-            in_copy(c, k).start()
-        return carry
-
-    lax.fori_loop(0, first, begin, 0)
-
     for e in range(1, n_dp):
         rs_copy(e).wait_recv()
     share = chosen[part(dp), :]
@@ -274,6 +283,7 @@
         sw_copy(s).start()
     for e in range(1, n_dp):
         ag_copy(0, e).start()
+    lax.fori_loop(early, first, begin, 0)
 
     lv_copy.wait()
     for k in range(1, members):
@@ -316,9 +326,13 @@
         ag_arrival(0, e).wait_recv()
 
     def step(c, carry):
-        @pl.when(c + WINDOW < count)
+        @pl.when(c + first < count)
         def _():
-            begin(c + WINDOW, 0)
+            begin(c + first, 0)
+
+        @pl.when(c + first >= count + 1)
+        def _():
+            give(c + first - count - 1)
 
         for s in range(1, families):
             @pl.when(c == min(s * blocks - 1, HOOK + s - 1))
@@ -349,12 +363,23 @@
         restored = product(head, tail, basis_head, basis_tail, NT)
         head, tail = halves(restored)
         inbuf[c] = product(lh[...], ll[...], head, tail, NN)
-        for k in range(1, members):
-            out_copy(c, k).start()
-        own_out_copy(c).start()
         return carry
 
     lax.fori_loop(0, count, step, 0)
+
+    given = first - 1
+    queue = list(range(given, count))
+
+    def give_next(number):
+        for _ in range(number):
+            if queue:
+                c = queue.pop(0)
+                if c - given >= 0 and c >= first:
+                    for k in range(1, members):
+                        out_copy(c - first, k).wait_send()
+                give(c)
+
+    give_next(1)
 
     mine = acc[:, :128]
     for j in range(1, BR // 128):
@@ -375,6 +400,8 @@
             sqbuf.at[2 * turn], sqbuf.at[2 * turn + 1], sq_send.at[turn], sq_recv.at[turn], d, m
         )
         copy.start()
+        if turn >= (n_dp - 1).bit_length():
+            give_next(3)
         copy.wait_recv()
         mine = mine + sqbuf[2 * turn + 1]
         turn += 1
@@ -386,20 +413,31 @@
             sq_send.at[turn + s - 1], sq_recv.at[turn + s - 1], dp, cousin(s, 1),
         )
         copy.start()
+    give_next(3)
     for s in range(1, families):
         remote(
             sqbuf.at[2 * turn], sqbuf.at[2 * turn + s],
             sq_send.at[turn + s - 1], sq_recv.at[turn + s - 1], dp, cousin(s, 1),
         ).wait_recv()
         whole = whole + sqbuf[2 * turn + s]
-    total[...] = whole
+    mean_square = jnp.sum(whole, keepdims=True) / (rows * n_dp * n_mp * span * n_mp)
+    facbuf[...] = jnp.broadcast_to(lax.rsqrt(mean_square + epsilon), facbuf.shape)
+    give_next(count)
 
     def finish(c, carry):
-        own_out_copy(c).wait()
+        factor = facbuf[0:1, :]
+        out[:, column(c, seat)] = inbuf[c, row_part(seat), :] * factor
         for k in range(1, members):
             in_copy(c, k).wait_send()
-            out_copy(c, k).wait_send()
             out_arrival(c, k).wait_recv()
+            there = column(c, flip(seat, k))
+            out[:, there] = out[:, there] * factor
+
+        @pl.when(c >= count - first)
+        def _():
+            for k in range(1, members):
+                out_copy(c, k).wait_send()
+
         return carry
 
     for r in range(len(bits)):
@@ -448,17 +486,14 @@
         others = max(families - 1, 1)
         anywhere = pl.BlockSpec(memory_space=pl.ANY)
         flops = 3 * 2 * BL * count * BR * (2 * BL + 2 * BR)
-        raw, total = pl.pallas_call(
+        return pl.pallas_call(
             functools.partial(kernel, n_dp, n_mp, rows, members, families, span, blocks),
-            out_shape=(
-                jax.ShapeDtypeStruct((rows, total_cols), F32),
-                jax.ShapeDtypeStruct((8, 128), F32),
-            ),
+            out_shape=pltpu.VMEM((rows, total_cols), F32),
             in_specs=[
                 anywhere, anywhere, anywhere, anywhere,
                 pl.BlockSpec(memory_space=pltpu.SMEM), anywhere,
             ],
-            out_specs=(anywhere, pl.BlockSpec(memory_space=pltpu.VMEM)),
+            out_specs=pl.BlockSpec(memory_space=pltpu.VMEM),
             scratch_shapes=[
                 pltpu.VMEM((count, BL, BR), F32),
                 pltpu.VMEM((BL, BL), F32),
@@ -474,8 +509,9 @@
                 pltpu.VMEM((families, span, BR), F32),
                 pltpu.VMEM((2 * rounds + families, 8, 128), F32),
                 pltpu.VMEM((8, BR), F32),
+                pltpu.VMEM((8, BR), F32),
                 dma((count, many)), dma((count, many)), dma((count, many)), dma((count, many)),
-                dma((count,)), dma((count,)),
+                dma((count,)),
                 dma((2, many)), dma((2, many)), dma((many,)), dma((many,)),
                 dma((n_dp - 1,)), dma((n_dp - 1,)),
                 dma((families, n_dp - 1)), dma((families, n_dp - 1)),
@@ -484,7 +520,7 @@
                 dma((4,)),
             ],
             compiler_params=pltpu.CompilerParams(
-                collective_id=0, has_side_effects=True, vmem_limit_bytes=60 * 2**20
+                collective_id=0, has_side_effects=True, vmem_limit_bytes=VMEM_MIB * 2**20
             ),
             cost_estimate=pl.CostEstimate(
                 flops=flops, bytes_accessed=4 * rows * total_cols * 4, transcendentals=0
@@ -493,8 +529,6 @@
             gradient, left_basis, left_values.reshape(1, rows), candidates, owner,
             right_values.reshape(1, span),
         )
-        mean_square = jnp.sum(total) / (rows * n_dp * n_mp * total_cols)
-        return raw * lax.rsqrt(mean_square + epsilon)
 
     in_specs = (
         P(("dp", "mp"), None),

time: 436 us -> 417 us (0.956)
  other arithmetic: 12.8 us -> 0 us
  Pallas kernels: 422 us -> 411 us
  local copies, waits for them, and re-layouts: 0 us -> 6.16 us
    mul x1 -> x0, other arithmetic: 11.6 us -> none  [on_device(): return raw * lax.rsqrt(mean_square + epsilon)]
    pallas_call x1, Pallas kernels: 422 us -> 411 us  [on_device(): pl.pallas_call(functools.partial(kernel, n_dp, n_mp, rows, members, famil...]
    unnamed x0 -> x1, local copies, waits for them, and re-layouts: none -> 6.16 us
where the time goes in v1:
time: 417 us
  Pallas kernels  411 us (99%)
  local copies, waits for them, and re-layouts  6.16 us (1%)
    pallas_call x1, Pallas kernels, on_device(): pl.pallas_call(functools.partial(kernel, n_dp, n_mp, rows, members, famil...  411 us

profile of v1, /device:TPU:0, one launch (start us, length us, event | category | flops | bytes accessed | tf_op | source)
XLA Modules:
  0.0 417.0 jit_solution(8076552357614077181)
XLA Ops:
  0.0 410.9 %shard_map.64 = f32[256,16384]{1,0:T(8,128)S(1)} custom-call(f32[256,16384]{1,0:T(8,128)} %grad.1, f32[256,1024]{1,0:T(8,128)} %left.1, f32[1,256]{1,0:T(1,128)} %bitcast.3, f32[1,2048,256]{2,1,0:T(8,128)} %cand.1, s32[8]{0:T(128)} %owner.1, f32[1,2048]{1,0:T(1,128)} %bitcast.2), custom_call_target="tpu_custom_call" | custom-call | flops 64424509440 | bytes 67108864 | tf_op jit(solution)/shard_map/pallas_call | solution.py:489
  410.9 6.2 %copy.8 = f32[256,16384]{1,0:T(8,128)} copy(f32[256,16384]{1,0:T(8,128)S(1)} %shard_map.64) | data formatting | bytes 33554432

commit v2 on v1

--- a/solution.py
+++ b/solution.py
@@ -9,8 +9,9 @@
 
 BL = 1024
 BR = 256
-AHEAD = 4
-EARLY = 2
+AHEAD = 8
+EARLY = 4
+TAIL = 4
 HOOK = 2
 VMEM_MIB = 44
 
@@ -137,6 +138,9 @@
             for k in range(members - 1, 0, -1):
                 action(k)
 
+    near = [k for k in range(1, members) if k & (k - 1) == 0]
+    far = [k for k in range(1, members) if k & (k - 1)]
+
     def give(c):
         each_peer(lambda k: out_copy(c, k).start())
 
@@ -213,10 +217,21 @@
         each_peer(lambda k: in_copy(c, k).start())
         return carry
 
+    def begin_near(c, carry):
+        own_in_copy(c).start()
+        for k in near:
+            in_copy(c, k).start()
+        return carry
+
+    def begin_far(c, carry):
+        for k in far:
+            in_copy(c, k).start()
+        return carry
+
     l_start(0)
     early = min(EARLY, count)
     first = min(AHEAD, count)
-    lax.fori_loop(0, early, begin, 0)
+    lax.fori_loop(0, early, begin_near, 0)
     for k in range(1, members):
         remote(
             lvals, lvbuf.at[seat], lv_send.at[k - 1], lv_recv.at[k - 1], dp, member(k)
@@ -272,6 +287,7 @@
         if r + 1 < len(bits):
             l_wait(r)
             l_start(r + 1)
+    lax.fori_loop(0, early, begin_far, 0)
 
     for e in range(1, n_dp):
         rs_copy(e).wait_recv()
@@ -369,6 +385,7 @@
 
     given = first - 1
     queue = list(range(given, count))
+    last = []
 
     def give_next(number):
         for _ in range(number):
@@ -377,7 +394,17 @@
                 if c - given >= 0 and c >= first:
                     for k in range(1, members):
                         out_copy(c - first, k).wait_send()
-                give(c)
+                if c < count - TAIL:
+                    give(c)
+                    continue
+                for k in far:
+                    out_copy(c, k).start()
+                last.append(c)
+        if not queue:
+            while last:
+                c = last.pop(0)
+                for k in near:
+                    out_copy(c, k).start()
 
     give_next(1)
 

time: 417 us -> 416 us (level)
  no operation moved by 1% of the time
where the time goes in v2:
time: 416 us
  Pallas kernels  410 us (99%)
  local copies, waits for them, and re-layouts  6.16 us (1%)
    pallas_call x1, Pallas kernels, on_device(): pl.pallas_call(functools.partial(kernel, n_dp, n_mp, rows, members, famil...  410 us

profile of v2, /device:TPU:0, one launch (start us, length us, event | category | flops | bytes accessed | tf_op | source)
XLA Modules:
  0.0 415.9 jit_solution(4531572423064664596)
XLA Ops:
  0.0 409.8 %shard_map.64 = f32[256,16384]{1,0:T(8,128)S(1)} custom-call(f32[256,16384]{1,0:T(8,128)} %grad.1, f32[256,1024]{1,0:T(8,128)} %left.1, f32[1,256]{1,0:T(1,128)} %bitcast.3, f32[1,2048,256]{2,1,0:T(8,128)} %cand.1, s32[8]{0:T(128)} %owner.1, f32[1,2048]{1,0:T(1,128)} %bitcast.2), custom_call_target="tpu_custom_call" | custom-call | flops 64424509440 | bytes 67108864 | tf_op jit(solution)/shard_map/pallas_call | solution.py:516
  409.8 6.2 %copy.8 = f32[256,16384]{1,0:T(8,128)} copy(f32[256,16384]{1,0:T(8,128)S(1)} %shard_map.64) | data formatting | bytes 33554432
